TPU v7x, 256 devices: a whole 4x4x8 slice. The times are simulated.
256 devices in a mesh: req: 16 (over y, x_hi, core), tp: 16 (over x_lo, z).
Axes of the slice: x: 4 (x_hi: 2, x_lo: 2; x = x_hi * 2 + x_lo), y: 4, z: 8, core: 2. Of those that a mesh axis runs over, the one named last changes fastest.
Arguments:
- patches: bfloat16 [16, 1024, 1664], P('req', 'tp'), may hold values from -6 to 6
- vis_gain: float32 [1664], replicated, may hold values from 0.1 to 1.9
- w_fc1: bfloat16 [1664, 8192], P(None, 'tp'), may hold values from -0.15625 to 0.15625
- w_fc2: bfloat16 [8192, 1664], P('tp'), may hold values from -0.125 to 0.125
- merge_gain: float32 [1664], replicated, may hold values from 0.1 to 1.9
- w_merge: bfloat16 [6656, 1664], P('tp'), may hold values from -0.078125 to 0.078125
- slots: int32 [16, 256], P('req'), may hold values from 0 to 3071, as said below
- text: bfloat16 [16, 3072, 1664], P('req', 'tp'), may hold values from -6 to 6
- docs: int32 [16, 3072], P('req'), may hold values from 0 to 7, never falling along the last dimension, each value on 1 to 768 neighbouring positions
- dec_gain: float32 [1664], replicated, may hold values from 0.1 to 1.9
- w_qkv: bfloat16 [1664, 4992], P(None, 'tp'), may hold values from -0.2773501 to 0.2773501
- w_out: bfloat16 [1664, 1664], P('tp'), may hold values from -0.625 to 0.625
Outputs:
- decoded: bfloat16 [16, 3072, 1664], P('req', 'tp')
Inputs may be any that keep to these rules, and one draw needn't show every extreme that they name: `slots`: positions in a group are distinct; each image's 64 merged rows take consecutive positions in order, and image k lies within positions j * 768 to (j + 1) * 768 - 1 with j = (k + 2) mod 4; the image with j = 3 takes the last 64 positions of the prompt. `docs`: request numbers never fall along a prompt; each request spans 1 to 768 positions.
All inputs are finite; a program needn't handle non-finite values.
Results may differ from a plain program's by a relative error of at most 0.033.
Values may be sent and summed in bfloat16 or wider, within the bound.
A program may use at most 64 MiB of HBM per device.

v0:
```python
import math
import jax
import jax.numpy as jnp
from jax import lax
from jax.sharding import PartitionSpec as P

HD = 104
EPSILON = 1e-06


def layer_norm(values, gains):
    average = jnp.mean(values, axis=-1, keepdims=True)
    centred = values - average
    variance = jnp.mean(centred * centred, axis=-1, keepdims=True)
    return centred * lax.rsqrt(variance + EPSILON) * gains


def rms_norm(values, gains):
    return values * lax.rsqrt(jnp.mean(values * values, axis=-1, keepdims=True) + EPSILON) * gains


def attend(qkv_rows, doc_row, heads_here):
    seq_len = qkv_rows.shape[0]
    block_rows = min(512, seq_len)
    shaped = qkv_rows.reshape(seq_len, heads_here, 3, HD)
    queries = shaped[:, :, 0]
    key_rows = shaped[:, :, 1]
    value_rows = shaped[:, :, 2]
    key_pos = jnp.arange(seq_len)

    def one_block(block_index):
        offset = block_index * block_rows
        query_block = lax.dynamic_slice_in_dim(queries, offset, block_rows, 0)
        query_pos = offset + jnp.arange(block_rows)
        query_docs = lax.dynamic_slice_in_dim(doc_row, offset, block_rows, 0)
        scores = jnp.einsum(
            "qhe,khe->hqk", query_block, key_rows, preferred_element_type=jnp.float32
        ) / math.sqrt(HD)
        allowed = (key_pos[None, :] <= query_pos[:, None]) & (
            doc_row[None, :] == query_docs[:, None]
        )
        scores = jnp.where(allowed[None], scores, -1e30)
        largest = jnp.max(scores, axis=-1, keepdims=True)
        raised = jnp.where(allowed[None], jnp.exp(scores - largest), 0.0)
        weights = (raised / jnp.sum(raised, axis=-1, keepdims=True)).astype(jnp.bfloat16)
        blended = jnp.einsum(
            "hqk,khe->qhe", weights, value_rows, preferred_element_type=jnp.float32
        )
        return blended.astype(jnp.bfloat16).reshape(block_rows, heads_here * HD)

    blocks = lax.map(one_block, jnp.arange(seq_len // block_rows))
    return blocks.reshape(seq_len, heads_here * HD)


def shards(
    patches, vis_gain, w_fc1, w_fc2, merge_gain, w_merge, slots, text, docs, dec_gain, w_qkv, w_out
):
    patch_rows = patches[0]
    slot_row = slots[0]
    text_rows = text[0]
    doc_row = docs[0]
    width = patch_rows.shape[1]
    local_rows = patch_rows.shape[0]
    seq_here = text_rows.shape[0]
    wide_in = patch_rows.astype(jnp.float32)
    normed_in = layer_norm(wide_in, vis_gain).astype(jnp.bfloat16)
    hidden = jax.nn.gelu(
        jnp.dot(
            lax.all_gather(normed_in, "tp", axis=0, tiled=True),
            w_fc1,
            preferred_element_type=jnp.float32,
        ),
        approximate=False,
    ).astype(jnp.bfloat16)
    mlp_sum = lax.psum_scatter(
        jnp.dot(hidden, w_fc2, preferred_element_type=jnp.float32).astype(jnp.bfloat16),
        "tp",
        scatter_dimension=0,
        tiled=True,
    ).astype(jnp.float32)
    normed_out = layer_norm(wide_in + mlp_sum, merge_gain).astype(jnp.bfloat16)
    merge_in = normed_out.reshape(local_rows // 4, 4 * width)
    features = lax.all_to_all(merge_in, "tp", split_axis=1, concat_axis=0, tiled=True)
    merge_term = jnp.dot(features, w_merge, preferred_element_type=jnp.float32)
    merged_share = lax.psum_scatter(
        merge_term.astype(jnp.bfloat16), "tp", scatter_dimension=0, tiled=True
    )
    merged = lax.all_gather(merged_share, "tp", axis=0, tiled=True)
    positions = lax.axis_index("tp") * seq_here + jnp.arange(seq_here, dtype=jnp.int32)
    matches = slot_row[None, :] == positions[:, None]
    placed = jnp.dot(
        matches.astype(jnp.bfloat16), merged, preferred_element_type=jnp.float32
    ).astype(jnp.bfloat16)
    embedded = jnp.where(jnp.any(matches, axis=1)[:, None], placed, text_rows)
    dec_in = rms_norm(embedded.astype(jnp.float32), dec_gain).astype(jnp.bfloat16)
    qkv_rows = jnp.dot(
        lax.all_gather(dec_in, "tp", axis=0, tiled=True), w_qkv, preferred_element_type=jnp.float32
    ).astype(jnp.bfloat16)
    heads_here = qkv_rows.shape[1] // (3 * HD)
    attended = attend(qkv_rows, doc_row, heads_here)
    out_sum = lax.psum_scatter(
        jnp.dot(attended, w_out, preferred_element_type=jnp.float32).astype(jnp.bfloat16),
        "tp",
        scatter_dimension=0,
        tiled=True,
    ).astype(jnp.float32)
    decoded = (embedded.astype(jnp.float32) + out_sum).astype(jnp.bfloat16)
    return decoded[None]


def solution(mesh):
    placed = (
        P("req", "tp", None),
        P(),
        P(None, "tp"),
        P("tp", None),
        P(),
        P("tp", None),
        P("req", None),
        P("req", "tp", None),
        P("req", None),
        P(),
        P(None, "tp"),
        P("tp", None),
    )
    return jax.shard_map(
        shards, mesh=mesh, in_specs=placed, out_specs=P("req", "tp", None), check_vma=False
    )
```

profile of v0, /device:TPU:1, one launch (start us, length us, event | category | flops | bytes accessed | tf_op | source)
XLA Modules:
  0.0 623.6 jit_solution(15786397968516002857)
XLA Ops:
  8.9 1.8 fusion.68
  10.8 70.4 %all-gather.3.cloned.1.call-done = bf16[1024,1664]{1,0:T(8,128)(2,1)} async-done(((bf16[64,1664]{1,0:T(8,128)(2,1)}), bf16[1024,1664]{1,0:T(8,128)(2,1)}) %all-gather.3.cloned.1.call-update) | async-done | bytes 3407888 | tf_op jit(solution)/shard_map/all_gather | solution.py:69
  81.1 11.6 %convolution_convert_fusion.2 = bf16[1024,1664]{1,0:T(8,128)(2,1)} fusion(bf16[512,1664]{1,0:T(8,128)(2,1)S(1)} %copy-done, bf16[1024,1664]{1,0:T(8,128)(2,1)} %all-gather.3.cloned.1.call-done, bf16[1664,512]{1,0:T(8,128)(2,1)} %param.16), kind=kOutput, calls=%fused_computation.24 | convolution fusion | flops 3525443584 | bytes 10223616 | tf_op jit(solution)/shard_map/dot_general | solution.py:76
  92.8 75.1 %reduce-scatter.4.cloned.1.call-done = bf16[64,1664]{1,0:T(8,128)(2,1)} async-done(((bf16[1024,1664]{1,0:T(8,128)(2,1)}), bf16[64,1664]{1,0:T(8,128)(2,1)}) %reduce-scatter.4.cloned.1.call-update) | async-done | bytes 213008 | tf_op jit(solution)/shard_map/reduce_scatter | solution.py:75
  171.7 10.4 %all_to_all.19 = bf16[16,16,416]{2,0,1:T(8,128)(2,1)S(1)} all-to-all(bf16[16,16,416]{2,0,1:T(8,128)(2,1)S(1)} %copy.18), channel_id=1, replica_groups=mesh['req'=16,'tp'=16] {'tp'}, dimensions={1} | all-to-all | bytes 425984 | tf_op jit(solution)/shard_map/all_to_all | solution.py:83
  182.1 2.9 convolution_convert_fusion.3
  185.3 68.8 %reduce-scatter.6.cloned.1.call-done = bf16[16,1664]{1,0:T(8,128)(2,1)} async-done(((bf16[256,1664]{1,0:T(8,128)(2,1)}), bf16[16,1664]{1,0:T(8,128)(2,1)}) %reduce-scatter.6.cloned.1.call-update) | async-done | bytes 53264 | tf_op jit(solution)/shard_map/reduce_scatter | solution.py:85
  254.1 30.6 %all_gather.10 = bf16[256,1664]{1,0:T(8,128)(2,1)S(1)} all-gather(bf16[16,1664]{1,0:T(8,128)(2,1)} %reduce-scatter.6.cloned.1.call-done), channel_id=1, replica_groups=mesh['req'=16,'tp'=16] {'tp'}, dimensions={0}, use_global_device_ids=true | all-gather | bytes 905216 | tf_op jit(solution)/shard_map/all_gather | solution.py:88
  287.6 132.2 %all-gather.5.cloned.1.call-done = bf16[3072,1664]{1,0:T(8,128)(2,1)} async-done(((bf16[192,1664]{1,0:T(8,128)(2,1)}), bf16[3072,1664]{1,0:T(8,128)(2,1)}) %all-gather.5.cloned.1.call-update) | async-done | bytes 10223632 | tf_op jit(solution)/shard_map/all_gather | solution.py:97
  419.8 7.8 %convolution_convert_fusion.1 = bf16[3072,312]{0,1:T(8,128)(2,1)S(1)} fusion(bf16[3072,1664]{1,0:T(8,128)(2,1)} %all-gather.5.cloned.1.call-done, bf16[1664,312]{0,1:T(8,128)(2,1)} %param.24), kind=kOutput, calls=%fused_computation.23 | convolution fusion | flops 3190726656 | bytes 13178880 | tf_op jit(solution)/shard_map/dot_general | solution.py:96
  428.9 61.9 %while.11 = (s32[]{:T(128)}, bf16[6,512,104]{1,2,0:T(8,128)(2,1)}, s32[6]{0:T(128)S(1)}, s32[1,3072]{1,0:T(1,128)S(1)}, s32[3072]{0:T(1024)S(1)}, /*index=5*/bf1...) while((s32[]{:T(128)}, bf16[6,512,104]{1,2,0:T(8,128)(2,1)}, ...), condition=%wide.region_11.12_spmd.clone, body=%wide.region_8.11_spmd.clone.sunk | while | flops 690540032 | bytes 22987480 | solution.py:51
  430.1 3.2 fusion.121
  433.3 2.5 fusion.122
  435.8 3.4 fusion.123
  440.4 3.2 fusion.121
  443.6 2.5 fusion.122
  446.2 3.4 fusion.123
  450.8 3.2 fusion.121
  453.9 2.5 fusion.122
  456.5 3.4 fusion.123
  461.1 3.2 fusion.121
  464.3 2.5 fusion.122
  466.8 3.4 fusion.123
  471.4 3.2 fusion.121
  474.6 2.5 fusion.122
  477.1 3.4 fusion.123
  481.7 3.2 fusion.121
  484.9 2.5 fusion.122
  487.5 3.4 fusion.123
  492.0 5.4 convolution_convert_fusion
  497.5 117.6 %reduce-scatter.8.cloned.1.call-done = bf16[192,1664]{1,0:T(8,128)(2,1)} async-done(((bf16[3072,1664]{1,0:T(8,128)(2,1)}), bf16[192,1664]{1,0:T(8,128)(2,1)}) %reduce-scatter.8.cloned.1.call-update) | async-done | bytes 638992 | tf_op jit(solution)/shard_map/reduce_scatter | solution.py:101
  615.0 2.0 fusion.61
  (74 shorter events, 15.7 us)
Async XLA Ops:
  6.5 74.6 %copy-start = (bf16[512,1664]{1,0:T(8,128)(2,1)S(1)}, bf16[512,1664]{1,0:T(8,128)(2,1)}, u32[]{:S(2)}) copy-start(bf16[512,1664]{1,0:T(8,128)(2,1)} %param.17) | copy-start | bytes 5111812
  6.5 74.6 %all-gather.3.cloned.1.call-start = ((), (), s32[]{:S(2)}) async-start(), calls=%async_computation.4 | async-start | bytes 3620864 | tf_op jit(solution)/shard_map/all_gather | solution.py:69
  10.7 157.2 %reduce-scatter.4.cloned.1.call-start = ((), (), s32[]{:S(2)}) async-start(), calls=%async_computation.5 | async-start | bytes 3620864 | tf_op jit(solution)/shard_map/reduce_scatter | solution.py:75
  92.7 75.2 %copy-start.1 = (bf16[1,64,1664]{2,1,0:T(8,128)(2,1)S(1)}, bf16[1,64,1664]{2,1,0:T(8,128)(2,1)}, u32[]{:S(2)}) copy-start(bf16[1,64,1664]{2,1,0:T(8,128)(2,1)} %param.14) | copy-start | bytes 638980
  92.7 77.5 %copy-start.5 = (f32[1664]{0:T(1024)S(1)}, f32[1664]{0:T(1024)}, u32[]{:S(2)}) copy-start(f32[1664]{0:T(1024)} %param.18) | copy-start | bytes 19972
  92.7 161.4 %reduce-scatter.6.cloned.1.call-start = ((), (), s32[]{:S(2)}) async-start(), calls=%async_computation.6 | async-start | bytes 905216 | tf_op jit(solution)/shard_map/reduce_scatter | solution.py:85
  171.6 13.5 %copy-start.7 = (s32[1,256]{1,0:T(1,128)S(1)}, s32[1,256]{1,0:T(1,128)}, u32[]{:S(2)}) copy-start(s32[1,256]{1,0:T(1,128)} %param.20) | copy-start | bytes 3076
  185.0 101.3 %copy-start.6 = (f32[1664]{0:T(1024)S(1)}, f32[1664]{0:T(1024)}, u32[]{:S(2)}) copy-start(f32[1664]{0:T(1024)} %param.23) | copy-start | bytes 19972
  185.0 234.8 %all-gather.5.cloned.1.call-start = ((), (), s32[]{:S(2)}) async-start(), calls=%async_computation.7 | async-start | bytes 10862592 | tf_op jit(solution)/shard_map/all_gather | solution.py:97
  287.4 327.7 %reduce-scatter.8.cloned.1.call-start = ((), (), s32[]{:S(2)}) async-start(), calls=%async_computation.8 | async-start | bytes 10862592 | tf_op jit(solution)/shard_map/reduce_scatter | solution.py:101
  427.6 1.3 copy-start.3
  428.9 63.1 %copy-start.4 = (bf16[104,1664]{1,0:T(8,128)(2,1)S(1)}, bf16[104,1664]{1,0:T(8,128)(2,1)}, u32[]{:S(2)}) copy-start(bf16[104,1664]{1,0:T(8,128)(2,1)} %param.25) | copy-start | bytes 1038340
  433.3 2.5 copy-start.2
  443.6 2.5 copy-start.2
  453.9 2.5 copy-start.2
  464.3 2.5 copy-start.2
  474.6 2.5 copy-start.2
  484.9 2.5 copy-start.2
Sparse Core Ops, SparseCore 0:
  10.8 70.2 all-gather.2
  92.9 75.0 reduce-scatter.3
  185.1 68.9 reduce-scatter.5
  287.5 132.2 all-gather.4
  497.6 117.3 reduce-scatter.7
where the time goes:
time: 624 us
  waiting for transfers between devices  464 us (74%)
  matrix products  68.8 us (11%)
  blocking collectives  41 us (7%)
  other arithmetic  25.9 us (4%)
  between operations  13.3 us (2%)
  local copies, waits for them, and re-layouts  6.75 us (1%)
    all_gather x1, waiting for transfers between devices, shards(): lax.all_gather(dec_in, 'tp', axis=0, tiled=True)  132 us
    reduce_scatter x1, waiting for transfers between devices, shards(): lax.psum_scatter(jnp.dot(attended, w_out, preferred_element_type=jnp.floa...  118 us
    reduce_scatter x1, waiting for transfers between devices, shards(): lax.psum_scatter(jnp.dot(hidden, w_fc2, preferred_element_type=jnp.float3...  75.1 us
    all_gather x1, waiting for transfers between devices, shards(): lax.all_gather(normed_in, 'tp', axis=0, tiled=True)  70.4 us
    reduce_scatter x1, waiting for transfers between devices, shards(): lax.psum_scatter(merge_term.astype(jnp.bfloat16), 'tp', scatter_dimension...  68.8 us
    all_gather x1, blocking collectives, shards(): merged = lax.all_gather(merged_share, 'tp', axis=0, tiled=True)  30.6 us
    dot_general x6, matrix products, one_block(): jnp.einsum('hqk,khe->qhe', weights, value_rows, preferred_element_type=jn...  20.5 us
    dot_general x6, matrix products, one_block(): jnp.einsum('qhe,khe->hqk', query_block, key_rows, preferred_element_type=...  19 us
  transfers between devices with their start and end apart: 5, of which 5 were waited for; matrix products, arithmetic and copies ran while one was open for 0% of the time, Pallas kernels for 0%

commit v1 on v0

--- a/solution.py
+++ b/solution.py
@@ -6,6 +6,14 @@
 
 HD = 104
 EPSILON = 1e-06
+
+
+def proceed_the_results(u):
+    current_block = lax.axis_size("tp")
+    raw_out = jnp.stack([u] * current_block, axis=0)
+    local_next = lax.all_to_all(raw_out, "tp", 0, 0)
+    carry_in = jnp.concatenate(local_next, axis=0)
+    return carry_in
 
 
 def layer_norm(values, gains):
@@ -94,7 +102,7 @@
     embedded = jnp.where(jnp.any(matches, axis=1)[:, None], placed, text_rows)
     dec_in = rms_norm(embedded.astype(jnp.float32), dec_gain).astype(jnp.bfloat16)
     qkv_rows = jnp.dot(
-        lax.all_gather(dec_in, "tp", axis=0, tiled=True), w_qkv, preferred_element_type=jnp.float32
+        proceed_the_results(dec_in), w_qkv, preferred_element_type=jnp.float32
     ).astype(jnp.bfloat16)
     heads_here = qkv_rows.shape[1] // (3 * HD)
     attended = attend(qkv_rows, doc_row, heads_here)

time: 624 us -> 726 us (1.16)
  waiting for transfers between devices: 464 us -> 556 us
    all_to_all x0 -> x1, waiting for transfers between devices: none -> 213 us  [proceed_the_results(): local_next = lax.all_to_all(raw_out, 'tp', 0, 0)]
    all_gather x1 -> x0, waiting for transfers between devices: 132 us -> none  [shards(): lax.all_gather(dec_in, 'tp', axis=0, tiled=True)]
    reduce_scatter x1, waiting for transfers between devices: 118 us -> 129 us  [shards(): lax.psum_scatter(jnp.dot(attended, w_out, preferred_element_type=jnp.floa...]
where the time goes in v1:
time: 726 us; the launch traced here: 725 us
  waiting for transfers between devices  556 us (77%)
  matrix products  67.5 us (9%)
  blocking collectives  41 us (6%)
  other arithmetic  25 us (3%)
  local copies, waits for them, and re-layouts  13.3 us (2%)
  between operations  13.3 us (2%)
    all_to_all x1, waiting for transfers between devices, proceed_the_results(): local_next = lax.all_to_all(raw_out, 'tp', 0, 0)  213 us
    reduce_scatter x1, waiting for transfers between devices, shards(): lax.psum_scatter(jnp.dot(attended, w_out, preferred_element_type=jnp.floa...  129 us
    reduce_scatter x1, waiting for transfers between devices, shards(): lax.psum_scatter(jnp.dot(hidden, w_fc2, preferred_element_type=jnp.float3...  75.1 us
    all_gather x1, waiting for transfers between devices, shards(): lax.all_gather(normed_in, 'tp', axis=0, tiled=True)  70.4 us
    reduce_scatter x1, waiting for transfers between devices, shards(): lax.psum_scatter(merge_term.astype(jnp.bfloat16), 'tp', scatter_dimension...  68.9 us
    all_gather x1, blocking collectives, shards(): merged = lax.all_gather(merged_share, 'tp', axis=0, tiled=True)  30.6 us
    dot_general x6, matrix products, one_block(): jnp.einsum('hqk,khe->qhe', weights, value_rows, preferred_element_type=jn...  20.5 us
    dot_general x6, matrix products, one_block(): jnp.einsum('qhe,khe->hqk', query_block, key_rows, preferred_element_type=...  19 us
  transfers between devices with their start and end apart: 5, of which 5 were waited for; matrix products, arithmetic and copies ran while one was open for 0% of the time, Pallas kernels for 0%

profile of v1, /device:TPU:1, one launch (start us, length us, event | category | flops | bytes accessed | tf_op | source)
XLA Modules:
  0.0 725.0 jit_solution(217852721181367010)
XLA Ops:
  10.8 70.4 %all-gather.2.cloned.1.call-done = bf16[1024,1664]{1,0:T(8,128)(2,1)} async-done(((bf16[64,1664]{1,0:T(8,128)(2,1)}), bf16[1024,1664]{1,0:T(8,128)(2,1)}) %all-gather.2.cloned.1.call-update) | async-done | bytes 3407888 | tf_op jit(solution)/shard_map/all_gather | solution.py:77
  81.1 11.6 %convolution_convert_fusion.2 = bf16[1024,1664]{1,0:T(8,128)(2,1)} fusion(bf16[512,1664]{1,0:T(8,128)(2,1)S(1)} %copy-done, bf16[1024,1664]{1,0:T(8,128)(2,1)} %all-gather.2.cloned.1.call-done, bf16[1664,512]{1,0:T(8,128)(2,1)} %param.16), kind=kOutput, calls=%fused_computation.24 | convolution fusion | flops 3525443584 | bytes 10223616 | tf_op jit(solution)/shard_map/dot_general | solution.py:84
  92.8 75.1 %reduce-scatter.4.cloned.1.call-done = bf16[64,1664]{1,0:T(8,128)(2,1)} async-done(((bf16[1024,1664]{1,0:T(8,128)(2,1)}), bf16[64,1664]{1,0:T(8,128)(2,1)}) %reduce-scatter.4.cloned.1.call-update) | async-done | bytes 213008 | tf_op jit(solution)/shard_map/reduce_scatter | solution.py:83
  173.4 10.4 %all_to_all.24 = bf16[16,16,416]{2,0,1:T(8,128)(2,1)S(1)} all-to-all(bf16[16,16,416]{2,0,1:T(8,128)(2,1)S(1)} %copy.18), channel_id=1, replica_groups=mesh['req'=16,'tp'=16] {'tp'}, dimensions={1} | all-to-all | bytes 425984 | tf_op jit(solution)/shard_map/all_to_all | solution.py:91
  185.6 68.9 %reduce-scatter.6.cloned.1.call-done = bf16[16,1664]{1,0:T(8,128)(2,1)} async-done(((bf16[256,1664]{1,0:T(8,128)(2,1)}), bf16[16,1664]{1,0:T(8,128)(2,1)}) %reduce-scatter.6.cloned.1.call-update) | async-done | bytes 53264 | tf_op jit(solution)/shard_map/reduce_scatter | solution.py:93
  254.4 30.6 %all_gather.7 = bf16[256,1664]{1,0:T(8,128)(2,1)S(1)} all-gather(bf16[16,1664]{1,0:T(8,128)(2,1)} %reduce-scatter.6.cloned.1.call-done), channel_id=1, replica_groups=mesh['req'=16,'tp'=16] {'tp'}, dimensions={0}, use_global_device_ids=true | all-gather | bytes 905216 | tf_op jit(solution)/shard_map/all_gather | solution.py:96
  286.8 4.9 stack.2
  291.7 4.8 all-to-all-start.1
  296.8 213.4 %all-to-all-done.1 = bf16[16,192,1664]{2,1,0:T(8,128)(2,1)} async-done(((bf16[16,192,1664]{2,1,0:T(8,128)(2,1)}), bf16[16,192,1664]{2,1,0:T(8,128)(2,1)}, u32[]{:S(2)}, u32[]{:S(2)}) %all-to-all-start.1) | async-done | bytes 10223648 | tf_op jit(solution)/shard_map/all_to_all | solution.py:14
  510.2 7.8 %convolution_convert_fusion.1 = bf16[3072,312]{0,1:T(8,128)(2,1)S(1)} fusion(bf16[3072,1664]{1,0:T(8,128)(2,1)} %bitcast.6, bf16[1664,312]{0,1:T(8,128)(2,1)} %param.24), kind=kOutput, calls=%fused_computation.23 | convolution fusion | flops 3190726656 | bytes 13178880 | tf_op jit(solution)/shard_map/dot_general | solution.py:104
  519.3 61.9 %while.11 = (s32[]{:T(128)}, bf16[6,512,104]{1,2,0:T(8,128)(2,1)}, s32[6]{0:T(128)S(1)}, s32[1,3072]{1,0:T(1,128)S(1)}, s32[3072]{0:T(1024)S(1)}, /*index=5*/bf1...) while((s32[]{:T(128)}, bf16[6,512,104]{1,2,0:T(8,128)(2,1)}, ...), condition=%wide.region_11.12_spmd.clone, body=%wide.region_8.11_spmd.clone.sunk | while | flops 690540032 | bytes 22987480 | solution.py:59
  520.5 3.2 fusion.121
  523.7 2.5 fusion.122
  526.2 3.4 fusion.123
  530.8 3.2 fusion.121
  534.0 2.5 fusion.122
  536.6 3.4 fusion.123
  541.2 3.2 fusion.121
  544.4 2.5 fusion.122
  546.9 3.4 fusion.123
  551.5 3.2 fusion.121
  554.7 2.5 fusion.122
  557.2 3.4 fusion.123
  561.8 3.2 fusion.121
  565.0 2.5 fusion.122
  567.5 3.4 fusion.123
  572.1 3.2 fusion.121
  575.3 2.5 fusion.122
  577.9 3.4 fusion.123
  582.4 5.4 convolution_convert_fusion
  587.9 128.5 %reduce-scatter.8.cloned.1.call-done = bf16[192,1664]{1,0:T(8,128)(2,1)} async-done(((bf16[3072,1664]{1,0:T(8,128)(2,1)}), bf16[192,1664]{1,0:T(8,128)(2,1)}) %reduce-scatter.8.cloned.1.call-update) | async-done | bytes 638992 | tf_op jit(solution)/shard_map/reduce_scatter | solution.py:109
  716.4 2.0 fusion.61
  (76 shorter events, 19.7 us)
Async XLA Ops:
  6.5 74.6 %copy-start = (bf16[512,1664]{1,0:T(8,128)(2,1)S(1)}, bf16[512,1664]{1,0:T(8,128)(2,1)}, u32[]{:S(2)}) copy-start(bf16[512,1664]{1,0:T(8,128)(2,1)} %param.17) | copy-start | bytes 5111812
  6.5 74.6 %all-gather.2.cloned.1.call-start = ((), (), s32[]{:S(2)}) async-start(), calls=%async_computation.5 | async-start | bytes 3620864 | tf_op jit(solution)/shard_map/all_gather | solution.py:77
  10.7 157.2 %reduce-scatter.4.cloned.1.call-start = ((), (), s32[]{:S(2)}) async-start(), calls=%async_computation.6 | async-start | bytes 3620864 | tf_op jit(solution)/shard_map/reduce_scatter | solution.py:83
  92.7 75.2 %copy-start.1 = (bf16[1,64,1664]{2,1,0:T(8,128)(2,1)S(1)}, bf16[1,64,1664]{2,1,0:T(8,128)(2,1)}, u32[]{:S(2)}) copy-start(bf16[1,64,1664]{2,1,0:T(8,128)(2,1)} %param.14) | copy-start | bytes 638980
  92.7 77.5 %copy-start.6 = (f32[1664]{0:T(1024)S(1)}, f32[1664]{0:T(1024)}, u32[]{:S(2)}) copy-start(f32[1664]{0:T(1024)} %param.18) | copy-start | bytes 19972
  92.7 91.0 %copy-start.2 = (bf16[416,1664]{1,0:T(8,128)(2,1)S(1)}, bf16[416,1664]{1,0:T(8,128)(2,1)}, u32[]{:S(2)}) copy-start(bf16[416,1664]{1,0:T(8,128)(2,1)} %param.19) | copy-start | bytes 4153348
  92.7 161.7 %reduce-scatter.6.cloned.1.call-start = ((), (), s32[]{:S(2)}) async-start(), calls=%async_computation.7 | async-start | bytes 905216 | tf_op jit(solution)/shard_map/reduce_scatter | solution.py:93
  172.3 13.1 %copy-start.8 = (s32[1,256]{1,0:T(1,128)S(1)}, s32[1,256]{1,0:T(1,128)}, u32[]{:S(2)}) copy-start(s32[1,256]{1,0:T(1,128)} %param.20) | copy-start | bytes 3076
  185.3 101.3 %copy-start.7 = (f32[1664]{0:T(1024)S(1)}, f32[1664]{0:T(1024)}, u32[]{:S(2)}) copy-start(f32[1664]{0:T(1024)} %param.23) | copy-start | bytes 19972
  291.7 218.5 %all-to-all-start.1 = ((bf16[16,192,1664]{2,1,0:T(8,128)(2,1)}), bf16[16,192,1664]{2,1,0:T(8,128)(2,1)}, u32[]{:S(2)}, u32[]{:S(2)}) async-start(bf16[16,192,1664]{2,1,0:T(8,128)(2,1)} %stack.2), calls=%async_computation.3 | async-start | bytes 20447232 | tf_op jit(solution)/shard_map/all_to_all | solution.py:14
  296.5 419.9 %reduce-scatter.8.cloned.1.call-start = ((), (), s32[]{:S(2)}) async-start(), calls=%async_computation.8 | async-start | bytes 10862592 | tf_op jit(solution)/shard_map/reduce_scatter | solution.py:109
  518.0 1.3 copy-start.4
  519.3 63.1 %copy-start.5 = (bf16[104,1664]{1,0:T(8,128)(2,1)S(1)}, bf16[104,1664]{1,0:T(8,128)(2,1)}, u32[]{:S(2)}) copy-start(bf16[104,1664]{1,0:T(8,128)(2,1)} %param.25) | copy-start | bytes 1038340
  523.7 2.5 copy-start.3
  534.0 2.5 copy-start.3
  544.3 2.5 copy-start.3
  554.7 2.5 copy-start.3
  565.0 2.5 copy-start.3
  575.3 2.5 copy-start.3
Sparse Core Ops, SparseCore 0:
  10.8 70.2 all-gather.1
  92.9 75.0 reduce-scatter.3
  185.5 68.9 reduce-scatter.5
  588.0 128.3 reduce-scatter.7
